TPU v7x, 32 devices: a whole 2x2x4 slice. The times are simulated.
32 devices in a mesh: tm: 2 (over x), grid: 16 (over z, y, core).
Axes of the slice: x: 2, y: 2, z: 4, core: 2. Of those that a mesh axis runs over, the one named last changes fastest.
Arguments:
- occupied_green: bfloat16 [2, 1024, 1024], P('tm', 'grid'), may hold values from -0.005859375 to 0.005859375
- empty_green: bfloat16 [2, 1024, 1024], P('tm', 'grid'), may hold values from -0.005859375 to 0.005859375
- basis: bfloat16 [12288, 1024], P('grid'), may hold values from -8 to 8
- time_weights: float32 [2, 2], replicated, may hold values from 0.25 to 1
Outputs:
- polarizability: float32 [2, 1024, 1024], P('tm', 'grid')
All inputs are finite; a program needn't handle non-finite values.
Results may differ from a plain program's by a relative error of at most 0.0012.
Values may be sent and summed in bfloat16 or wider, within the bound.
A program may use at most 128 MiB of HBM per device.

v0:
```python
import jax
import jax.numpy as jnp
from jax import lax
from jax.sharding import PartitionSpec as P

NR = 12288
NB = 1024


def weigh_times(time_weights, block_list, scale_factor):
    time_count = len(block_list)
    group_index = lax.axis_index("tm")
    weights_local = lax.dynamic_slice_in_dim(time_weights, group_index * time_count, time_count, 1)
    accum = weights_local[:, 0, None, None] * block_list[0][None]
    return scale_factor * accum


def step_size(piece_rows):
    return max((divisor for divisor in range(1, 2049) if piece_rows % divisor == 0))


def shards(occupied_green, empty_green, basis, time_weights):
    stacked = jnp.stack([occupied_green, empty_green])
    time_count = occupied_green.shape[0]
    coef_block = occupied_green.shape[1]
    row_total = basis.shape[0]
    scale_factor = 1.0 / NR

    def make_accumulate(combined_rows):

        def accumulate(running, basis_piece, first_row):
            piece_rows = basis_piece.shape[0]
            step_rows = step_size(piece_rows)

            def one_step(step_index, inner):
                basis_subpart = lax.dynamic_slice_in_dim(
                    basis_piece, step_index * step_rows, step_rows, 0
                )
                real_pair = jnp.einsum(
                    "qoa,ba->qob", combined_rows, basis_subpart, preferred_element_type=jnp.float32
                )
                product = (real_pair[0] * real_pair[1]).astype(jnp.bfloat16)
                return inner + jnp.dot(product, basis_subpart, preferred_element_type=jnp.float32)

            return lax.fori_loop(0, piece_rows // step_rows, one_step, running)

        return accumulate

    initial = jnp.zeros((time_count * row_total, NB), jnp.float32)
    projected = jnp.einsum(
        "sl,ftkl->ftsk",
        basis,
        lax.all_gather(stacked, "grid", axis=2, tiled=True),
        preferred_element_type=jnp.float32,
    ).astype(jnp.bfloat16)
    combined_rows = projected.reshape(2, time_count * row_total, NB)
    accumulate = make_accumulate(combined_rows)
    summed = accumulate(initial, lax.all_gather(basis, "grid", axis=0, tiled=True), jnp.int32(0))
    back_half = summed.astype(jnp.bfloat16).reshape(time_count, row_total, NB)
    coef_rows = lax.psum_scatter(
        jnp.einsum("tsk,sl->ktl", back_half, basis, preferred_element_type=jnp.float32).reshape(
            lax.axis_size("grid") * coef_block, time_count * NB
        ),
        "grid",
        scatter_dimension=0,
        tiled=True,
    ).reshape(coef_block, time_count, NB)
    block_list = [coef_rows[:, 0]]
    result = lax.psum_scatter(
        weigh_times(time_weights, block_list, scale_factor), "tm", scatter_dimension=0, tiled=True
    )
    return result


def solution(mesh):
    in_specs = (P("tm", "grid", None), P("tm", "grid", None), P("grid", None), P())
    out_specs = P("tm", "grid", None)
    return jax.shard_map(shards, mesh=mesh, in_specs=in_specs, out_specs=out_specs, check_vma=False)
```

profile of v0, /device:TPU:0, one launch (start us, length us, event | category | flops | bytes accessed | tf_op | source)
XLA Modules:
  0.0 431.6 jit_solution(16188916720244867342)
XLA Ops:
  6.5 0.0 copy-start
  6.5 0.0 all-gather.5.cloned.1.call-start
  6.5 1.7 pad_maximum_fusion
  8.2 0.0 all-gather.5.cloned.1.call-update
  8.3 0.0 all-gather.3.cloned.1.call-start
  8.3 0.7 all-gather.3.cloned.1.call-update
  9.0 0.0 reduce-scatter.3.cloned.1.call-start
  9.1 53.6 %all-gather.5.cloned.1.call-done = bf16[2,1,1024,1024]{3,2,0,1:T(8,128)(2,1)} async-done(((bf16[2,1,64,1024]{3,2,0,1:T(8,128)(2,1)}), bf16[2,1,1024,1024]{3,2,0,1:T(8,128)(2,1)}) %all-gather.5.cloned.1.call-update) | async-done | bytes 4194320 | tf_op jit(solution)/shard_map/all_gather | solution.py:53
  62.7 7.9 %convert_bitcast_fusion = bf16[2,768,1024]{1,2,0:T(8,128)(2,1)} fusion(bf16[2,1,1024,1024]{3,2,0,1:T(8,128)(2,1)} %all-gather.5.cloned.1.call-done, bf16[768,1024]{1,0:T(8,128)(2,1)} %param.8), kind=kOutput, calls=%fused_computation.13 | convolution fusion | flops 3222798336 | bytes 8912896 | tf_op jit(solution)/shard_map/sl,ftkl->ftsk/dot_general | solution.py:50
  70.5 3.2 copy.5
  73.8 117.6 %all-gather.3.cloned.1.call-done = bf16[12288,1024]{1,0:T(8,128)(2,1)} async-done(((bf16[768,1024]{1,0:T(8,128)(2,1)}), bf16[12288,1024]{1,0:T(8,128)(2,1)}) %all-gather.3.cloned.1.call-update) | async-done | bytes 25165840 | tf_op jit(solution)/shard_map/all_gather | solution.py:58
  191.3 138.8 %while.14 = (s32[]{:T(128)}, f32[768,1024]{1,0:T(8,128)}, bf16[12288,1024]{1,0:T(8,128)(2,1)}, bf16[2,768,1024]{2,1,0:T(8,128)(2,1)S(1)}, s32[]{:T(128)}, /*index=5*/s32[]{:T(128)}, s32[]{:T(128)}, s32[]{:T(128)}) while((s32[]{:T(128)}, f32[768,1024]{1,0:T(8,128)}, bf16[12288,1024]{1,0:T(8,128)(2,1)}, ...), condition=%wide.region_1.0_spmd.clone, body=%wide.region_0.0_spmd.clone.sunk | while | flops 9668395008 | bytes 42991772 | solution.py:45
  191.4 11.5 %convolution_bitcast_fusion.2 = f32[2,768,2048]{1,2,0:T(8,128)} fusion(bf16[2,768,1024]{2,1,0:T(8,128)(2,1)S(1)} %get-tuple-element.156, bf16[12288,1024]{1,0:T(8,128)(2,1)} %get-tuple-element.155, s32[]{:T(128)S(6)} %select_n.13), kind=kOutput, calls=%fused_computation.2.clone.1 | convolution fusion | flops 6442450944 | bytes 19922948 | tf_op jit(solution)/shard_map/while/body/eval_jaxpr/qoa,ba->qob/dot_general | solution.py:39
  202.9 10.9 %select_add_fusion.2 = f32[768,1024]{1,0:T(8,128)} fusion(f32[768,1024]{1,0:T(8,128)} %get-tuple-element.146, bf16[12288,1024]{1,0:T(8,128)(2,1)} %get-tuple-element.155, s32[]{:T(128)S(6)} %select_n.13, f32[2,768,2048]{1,2,0:T(8,128)} %convolution_bitcast_fusion.2, pred[]{:T(512)S(6)} %compare.3), kind=kOutput, calls=%fused_computation.8.clone.1 | convolution fusion | flops 3225944064 | bytes 23068676 | tf_op jit(solution)/shard_map/while/body/eval_jaxpr/dot_general | solution.py:43
  213.7 11.5 %convolution_bitcast_fusion.2 = f32[2,768,2048]{1,2,0:T(8,128)} fusion(bf16[2,768,1024]{2,1,0:T(8,128)(2,1)S(1)} %get-tuple-element.156, bf16[12288,1024]{1,0:T(8,128)(2,1)} %get-tuple-element.155, s32[]{:T(128)S(6)} %select_n.13), kind=kOutput, calls=%fused_computation.2.clone.1 | convolution fusion | flops 6442450944 | bytes 19922948 | tf_op jit(solution)/shard_map/while/body/eval_jaxpr/qoa,ba->qob/dot_general | solution.py:39
  225.2 11.8 %select_add_fusion.2 = f32[768,1024]{1,0:T(8,128)} fusion(f32[768,1024]{1,0:T(8,128)} %get-tuple-element.146, bf16[12288,1024]{1,0:T(8,128)(2,1)} %get-tuple-element.155, s32[]{:T(128)S(6)} %select_n.13, f32[2,768,2048]{1,2,0:T(8,128)} %convolution_bitcast_fusion.2, pred[]{:T(512)S(6)} %compare.3), kind=kOutput, calls=%fused_computation.8.clone.1 | convolution fusion | flops 3225944064 | bytes 23068676 | tf_op jit(solution)/shard_map/while/body/eval_jaxpr/dot_general | solution.py:43
  237.0 11.5 %convolution_bitcast_fusion.2 = f32[2,768,2048]{1,2,0:T(8,128)} fusion(bf16[2,768,1024]{2,1,0:T(8,128)(2,1)S(1)} %get-tuple-element.156, bf16[12288,1024]{1,0:T(8,128)(2,1)} %get-tuple-element.155, s32[]{:T(128)S(6)} %select_n.13), kind=kOutput, calls=%fused_computation.2.clone.1 | convolution fusion | flops 6442450944 | bytes 19922948 | tf_op jit(solution)/shard_map/while/body/eval_jaxpr/qoa,ba->qob/dot_general | solution.py:39
  248.5 11.8 %select_add_fusion.2 = f32[768,1024]{1,0:T(8,128)} fusion(f32[768,1024]{1,0:T(8,128)} %get-tuple-element.146, bf16[12288,1024]{1,0:T(8,128)(2,1)} %get-tuple-element.155, s32[]{:T(128)S(6)} %select_n.13, f32[2,768,2048]{1,2,0:T(8,128)} %convolution_bitcast_fusion.2, pred[]{:T(512)S(6)} %compare.3), kind=kOutput, calls=%fused_computation.8.clone.1 | convolution fusion | flops 3225944064 | bytes 23068676 | tf_op jit(solution)/shard_map/while/body/eval_jaxpr/dot_general | solution.py:43
  260.3 11.5 %convolution_bitcast_fusion.2 = f32[2,768,2048]{1,2,0:T(8,128)} fusion(bf16[2,768,1024]{2,1,0:T(8,128)(2,1)S(1)} %get-tuple-element.156, bf16[12288,1024]{1,0:T(8,128)(2,1)} %get-tuple-element.155, s32[]{:T(128)S(6)} %select_n.13), kind=kOutput, calls=%fused_computation.2.clone.1 | convolution fusion | flops 6442450944 | bytes 19922948 | tf_op jit(solution)/shard_map/while/body/eval_jaxpr/qoa,ba->qob/dot_general | solution.py:39
  271.8 11.8 %select_add_fusion.2 = f32[768,1024]{1,0:T(8,128)} fusion(f32[768,1024]{1,0:T(8,128)} %get-tuple-element.146, bf16[12288,1024]{1,0:T(8,128)(2,1)} %get-tuple-element.155, s32[]{:T(128)S(6)} %select_n.13, f32[2,768,2048]{1,2,0:T(8,128)} %convolution_bitcast_fusion.2, pred[]{:T(512)S(6)} %compare.3), kind=kOutput, calls=%fused_computation.8.clone.1 | convolution fusion | flops 3225944064 | bytes 23068676 | tf_op jit(solution)/shard_map/while/body/eval_jaxpr/dot_general | solution.py:43
  283.6 11.5 %convolution_bitcast_fusion.2 = f32[2,768,2048]{1,2,0:T(8,128)} fusion(bf16[2,768,1024]{2,1,0:T(8,128)(2,1)S(1)} %get-tuple-element.156, bf16[12288,1024]{1,0:T(8,128)(2,1)} %get-tuple-element.155, s32[]{:T(128)S(6)} %select_n.13), kind=kOutput, calls=%fused_computation.2.clone.1 | convolution fusion | flops 6442450944 | bytes 19922948 | tf_op jit(solution)/shard_map/while/body/eval_jaxpr/qoa,ba->qob/dot_general | solution.py:39
  295.1 11.8 %select_add_fusion.2 = f32[768,1024]{1,0:T(8,128)} fusion(f32[768,1024]{1,0:T(8,128)} %get-tuple-element.146, bf16[12288,1024]{1,0:T(8,128)(2,1)} %get-tuple-element.155, s32[]{:T(128)S(6)} %select_n.13, f32[2,768,2048]{1,2,0:T(8,128)} %convolution_bitcast_fusion.2, pred[]{:T(512)S(6)} %compare.3), kind=kOutput, calls=%fused_computation.8.clone.1 | convolution fusion | flops 3225944064 | bytes 23068676 | tf_op jit(solution)/shard_map/while/body/eval_jaxpr/dot_general | solution.py:43
  306.9 11.5 %convolution_bitcast_fusion.2 = f32[2,768,2048]{1,2,0:T(8,128)} fusion(bf16[2,768,1024]{2,1,0:T(8,128)(2,1)S(1)} %get-tuple-element.156, bf16[12288,1024]{1,0:T(8,128)(2,1)} %get-tuple-element.155, s32[]{:T(128)S(6)} %select_n.13), kind=kOutput, calls=%fused_computation.2.clone.1 | convolution fusion | flops 6442450944 | bytes 19922948 | tf_op jit(solution)/shard_map/while/body/eval_jaxpr/qoa,ba->qob/dot_general | solution.py:39
  318.4 11.8 %select_add_fusion.2 = f32[768,1024]{1,0:T(8,128)} fusion(f32[768,1024]{1,0:T(8,128)} %get-tuple-element.146, bf16[12288,1024]{1,0:T(8,128)(2,1)} %get-tuple-element.155, s32[]{:T(128)S(6)} %select_n.13, f32[2,768,2048]{1,2,0:T(8,128)} %convolution_bitcast_fusion.2, pred[]{:T(512)S(6)} %compare.3), kind=kOutput, calls=%fused_computation.8.clone.1 | convolution fusion | flops 3225944064 | bytes 23068676 | tf_op jit(solution)/shard_map/while/body/eval_jaxpr/dot_general | solution.py:43
  330.2 6.1 %fusion.18 = f32[1024,1024]{1,0:T(8,128)} fusion(bf16[768,1024]{1,0:T(8,128)(2,1)} %param.8, f32[768,1024]{1,0:T(8,128)} %get-tuple-element.84), kind=kOutput, calls=%fused_computation.15 | convolution fusion | flops 1611399168 | bytes 8912896 | tf_op jit(solution)/shard_map/tsk,sl->ktl/dot_general | solution.py:61
  336.3 0.0 reduce-scatter.3.cloned.1.call-update
  336.3 0.0 reduce-scatter.5.cloned.1.call-start
  336.4 0.0 copy-done
  336.4 0.2 dynamic-slice_reduce_fusion
  336.6 72.7 %reduce-scatter.3.cloned.1.call-done = f32[64,1024]{1,0:T(8,128)} async-done(((f32[1024,1024]{1,0:T(8,128)}), f32[64,1024]{1,0:T(8,128)}) %reduce-scatter.3.cloned.1.call-update) | async-done | bytes 262160 | tf_op jit(solution)/shard_map/reduce_scatter | solution.py:60
  409.2 1.9 multiply_multiply_fusion
  411.1 0.0 reduce-scatter.5.cloned.1.call-update
  411.1 13.9 %reduce-scatter.5.cloned.1.call-done = f32[1,64,1024]{2,1,0:T(8,128)} async-done(((f32[2,64,1024]{2,1,0:T(8,128)}), f32[1,64,1024]{2,1,0:T(8,128)}) %reduce-scatter.5.cloned.1.call-update) | async-done | bytes 262160 | tf_op jit(solution)/shard_map/reduce_scatter | solution.py:69
  (1 shorter events, 0.0 us)
Async XLA Ops:
  6.5 329.8 %copy-start = (f32[2,2]{1,0:T(2,128)S(1)}, f32[2,2]{1,0:T(2,128)}, u32[]{:S(2)}) copy-start(f32[2,2]{1,0:T(2,128)} %param.9) | copy-start | bytes 52
  6.5 56.1 %all-gather.5.cloned.1.call-start = ((), (), s32[]{:S(2)}) async-start(), calls=%async_computation.3 | async-start | bytes 4456448 | tf_op jit(solution)/shard_map/all_gather | solution.py:53
  8.3 183.1 %all-gather.3.cloned.1.call-start = ((), (), s32[]{:S(2)}) async-start(), calls=%async_computation.2 | async-start | bytes 26738688 | tf_op jit(solution)/shard_map/all_gather | solution.py:58
  9.0 400.2 %reduce-scatter.3.cloned.1.call-start = ((), (), s32[]{:S(2)}) async-start(), calls=%async_computation.4 | async-start | bytes 4456448 | tf_op jit(solution)/shard_map/reduce_scatter | solution.py:60
  336.3 88.8 %reduce-scatter.5.cloned.1.call-start = ((), (), s32[]{:S(2)}) async-start(), calls=%async_computation.5 | async-start | bytes 786432 | tf_op jit(solution)/shard_map/reduce_scatter | solution.py:69
Sparse Core Ops, SparseCore 0:
  9.5 53.1 all-gather.4
  64.3 127.0 all-gather.2
  336.4 72.7 reduce-scatter.2
  411.3 13.6 reduce-scatter.4
where the time goes:
time: 432 us
  waiting for transfers between devices  259 us (60%)
  matrix products  153 us (35%)
  between operations  13.2 us (3%)
    all_gather x1, waiting for transfers between devices, shards(): lax.all_gather(basis, 'grid', axis=0, tiled=True)  118 us
    reduce_scatter x1, waiting for transfers between devices, shards(): lax.psum_scatter(jnp.einsum('tsk,sl->ktl', back_half, basis, preferred_el...  72.7 us
    dot_general x6, matrix products, one_step(): jnp.dot(product, basis_subpart, preferred_element_type=jnp.float32)  69.8 us
    dot_general x6, matrix products, one_step(): jnp.einsum('qoa,ba->qob', combined_rows, basis_subpart, preferred_element...  69 us
    all_gather x1, waiting for transfers between devices, shards(): lax.all_gather(stacked, 'grid', axis=2, tiled=True)  53.6 us
    reduce_scatter x1, waiting for transfers between devices, shards(): lax.psum_scatter(weigh_times(time_weights, block_list, scale_factor), 'tm...  13.9 us
  transfers between devices with their start and end apart: 4, of which 4 were waited for; matrix products, arithmetic and copies ran while one was open for 3% of the time, Pallas kernels for 0%

commit v1 on v0

--- a/solution.py
+++ b/solution.py
@@ -5,6 +5,30 @@
 
 NR = 12288
 NB = 1024
+
+
+def kinds_begin(tile_in, my_data):
+    carry = lax.axis_size("grid")
+    u_next = lax.axis_index("grid")
+    z2, val2, u1 = (carry, u_next, tile_in.shape[2])
+    so_far_all = []
+    for u in range(z2):
+        so_far_all.append((u, (u + 1) % z2))
+    tmp, moved = (tile_in, None)
+    for s in range(z2):
+        current_block = (val2 - s) % z2
+        z = lax.ppermute(tmp, "grid", so_far_all) if s < z2 - 1 else None
+        shaped = my_data(tmp, current_block * u1)
+        current_value = shaped.shape[3]
+        if moved is None:
+            moved = jnp.zeros(
+                (*shaped.shape[:3], z2 * current_value, *shaped.shape[4:]), shaped.dtype
+            )
+        moved = lax.dynamic_update_slice_in_dim(
+            moved, shaped, current_block * current_value, axis=3
+        )
+        tmp = z
+    return moved
 
 
 def weigh_times(time_weights, block_list, scale_factor):
@@ -47,11 +71,11 @@
         return accumulate
 
     initial = jnp.zeros((time_count * row_total, NB), jnp.float32)
-    projected = jnp.einsum(
-        "sl,ftkl->ftsk",
-        basis,
-        lax.all_gather(stacked, "grid", axis=2, tiled=True),
-        preferred_element_type=jnp.float32,
+    projected = kinds_begin(
+        stacked,
+        lambda own_block, at: jnp.einsum(
+            "sl,ftkl->ftsk", basis, own_block, preferred_element_type=jnp.float32
+        ),
     ).astype(jnp.bfloat16)
     combined_rows = projected.reshape(2, time_count * row_total, NB)
     accumulate = make_accumulate(combined_rows)

time: 432 us -> 435 us (level)
  local copies, waits for them, and re-layouts: 3.4 us -> 111 us
  waiting for transfers between devices: 259 us -> 190 us
  matrix products: 153 us -> 112 us
    all_gather x1, waiting for transfers between devices: 118 us -> 0.01 us  [shards(): lax.all_gather(basis, 'grid', axis=0, tiled=True)]
    ppermute x0 -> x15, waiting for transfers between devices: none -> 100 us  [kinds_begin(): z = lax.ppermute(tmp, 'grid', so_far_all) if s < z2 - 1 else None]
    dynamic_update_slice x0 -> x16, local copies, waits for them, and re-layouts: none -> 93.8 us  [kinds_begin(): lax.dynamic_update_slice_in_dim(moved, shaped, current_block * current_va...]
    all_gather x1 -> x0, waiting for transfers between devices: 53.6 us -> none  [shards(): lax.all_gather(stacked, 'grid', axis=2, tiled=True)]
    dot_general x6, matrix products: 69.8 us -> 33.9 us  [one_step(): jnp.dot(product, basis_subpart, preferred_element_type=jnp.float32)]
    dot_general x6, matrix products: 69 us -> 57.6 us  [one_step(): jnp.einsum('qoa,ba->qob', combined_rows, basis_subpart, preferred_element...]
    while x0 -> x24, local copies, waits for them, and re-layouts: none -> 10.1 us
    dot_general x1 -> x16, matrix products: 7.87 us -> 15.2 us  [shards(): jnp.einsum('sl,ftkl->ftsk', basis, own_block, preferred_element_type=jnp....]
  transfers between devices with their start and end apart: 4 -> 18, of which waited for: 4 -> 12; matrix products, arithmetic and copies ran while one was open for 3% -> 27% of each run, Pallas kernels for 0% -> 0%
where the time goes in v1:
time: 435 us; the launch traced here: 431 us
  waiting for transfers between devices  190 us (44%)
  matrix products  112 us (26%)
  local copies, waits for them, and re-layouts  111 us (26%)
  between operations  13.5 us (3%)
    ppermute x15, waiting for transfers between devices, kinds_begin(): z = lax.ppermute(tmp, 'grid', so_far_all) if s < z2 - 1 else None  100 us
    dynamic_update_slice x16, local copies, waits for them, and re-layouts, kinds_begin(): lax.dynamic_update_slice_in_dim(moved, shaped, current_block * current_va...  93.8 us
    reduce_scatter x1, waiting for transfers between devices, shards(): lax.psum_scatter(jnp.einsum('tsk,sl->ktl', back_half, basis, preferred_el...  75.7 us
    dot_general x6, matrix products, one_step(): jnp.einsum('qoa,ba->qob', combined_rows, basis_subpart, preferred_element...  57.6 us
    dot_general x6, matrix products, one_step(): jnp.dot(product, basis_subpart, preferred_element_type=jnp.float32)  33.9 us
    dot_general x16, matrix products, shards(): jnp.einsum('sl,ftkl->ftsk', basis, own_block, preferred_element_type=jnp....  15.2 us
    reduce_scatter x1, waiting for transfers between devices, shards(): lax.psum_scatter(weigh_times(time_weights, block_list, scale_factor), 'tm...  14.1 us
    while x24, local copies, waits for them, and re-layouts  10.1 us
  transfers between devices with their start and end apart: 18, of which 12 were waited for; matrix products, arithmetic and copies ran while one was open for 27% of the time, Pallas kernels for 0%

profile of v1, /device:TPU:0, one launch (start us, length us, event | category | flops | bytes accessed | tf_op | source)
XLA Modules:
  0.0 431.3 jit_solution(16850558769675127698)
XLA Ops:
  6.6 0.7 all-gather.2.cloned.1.call-update
  7.3 1.0 pad_maximum_fusion
  8.9 9.0 %collective-permute-done = bf16[2,1,64,1024]{3,2,0,1:T(8,128)(2,1)S(1)} collective-permute-done((bf16[2,1,64,1024]{3,2,0,1:T(8,128)(2,1)S(1)}, bf16[2,1,64,1024]{3,2,0,1:T(8,128)(2,1)S(1)}, u32[]{:S(2)}, u32[]{:S(2)}) %collective-permute-start) | collective-permute-done | bytes 262176 | tf_op jit(solution)/shard_map/ppermute | solution.py:20
  17.9 0.7 copy-done.7
  18.6 13.2 %collective-permute-done.1 = bf16[2,1,64,1024]{3,2,0,1:T(8,128)(2,1)S(1)} collective-permute-done((bf16[2,1,64,1024]{3,2,0,1:T(8,128)(2,1)S(1)}, bf16[2,1,64,1024]{3,2,0,1:T(8,128)(2,1)S(1)}, u32[]{:S(2)}, u32[]{:S(2)}) %collective-permute-start.1) | collective-permute-done | bytes 262176 | tf_op jit(solution)/shard_map/ppermute | solution.py:20
  31.8 0.7 copy-done.9
  32.5 13.5 %collective-permute-done.2 = bf16[2,1,64,1024]{3,2,0,1:T(8,128)(2,1)S(1)} collective-permute-done((bf16[2,1,64,1024]{3,2,0,1:T(8,128)(2,1)S(1)}, bf16[2,1,64,1024]{3,2,0,1:T(8,128)(2,1)S(1)}, u32[]{:S(2)}, u32[]{:S(2)}) %collective-permute-start.2) | collective-permute-done | bytes 262176 | tf_op jit(solution)/shard_map/ppermute | solution.py:20
  46.0 14.2 %collective-permute-done.3 = bf16[2,1,64,1024]{3,2,0,1:T(8,128)(2,1)S(1)} collective-permute-done((bf16[2,1,64,1024]{3,2,0,1:T(8,128)(2,1)S(1)}, bf16[2,1,64,1024]{3,2,0,1:T(8,128)(2,1)S(1)}, u32[]{:S(2)}, u32[]{:S(2)}) %collective-permute-start.3) | collective-permute-done | bytes 262176 | tf_op jit(solution)/shard_map/ppermute | solution.py:20
  60.3 14.2 %collective-permute-done.4 = bf16[2,1,64,1024]{3,2,0,1:T(8,128)(2,1)S(1)} collective-permute-done((bf16[2,1,64,1024]{3,2,0,1:T(8,128)(2,1)S(1)}, bf16[2,1,64,1024]{3,2,0,1:T(8,128)(2,1)S(1)}, u32[]{:S(2)}, u32[]{:S(2)}) %collective-permute-start.4) | collective-permute-done | bytes 262176 | tf_op jit(solution)/shard_map/ppermute | solution.py:20
  74.5 14.2 %collective-permute-done.5 = bf16[2,1,64,1024]{3,2,0,1:T(8,128)(2,1)S(1)} collective-permute-done((bf16[2,1,64,1024]{3,2,0,1:T(8,128)(2,1)S(1)}, bf16[2,1,64,1024]{3,2,0,1:T(8,128)(2,1)S(1)}, u32[]{:S(2)}, u32[]{:S(2)}) %collective-permute-start.5) | collective-permute-done | bytes 262176 | tf_op jit(solution)/shard_map/ppermute | solution.py:20
  88.7 14.2 %collective-permute-done.6 = bf16[2,1,64,1024]{3,2,0,1:T(8,128)(2,1)S(1)} collective-permute-done((bf16[2,1,64,1024]{3,2,0,1:T(8,128)(2,1)S(1)}, bf16[2,1,64,1024]{3,2,0,1:T(8,128)(2,1)S(1)}, u32[]{:S(2)}, u32[]{:S(2)}) %collective-permute-start.6) | collective-permute-done | bytes 262176 | tf_op jit(solution)/shard_map/ppermute | solution.py:20
  103.0 0.7 fusion.47
  104.0 2.1 broadcast_in_dim.7
  106.1 5.5 %dynamic_update_slice.48 = bf16[2,1,768,1024]{3,2,0,1:T(8,128)(2,1)} dynamic-update-slice(bf16[2,1,768,1024]{3,2,0,1:T(8,128)(2,1)} %broadcast_in_dim.7, bf16[2,1,768,64]{3,2,0,1:T(8,128)(2,1)S(1)} %copy.5, s32[]{:T(128)} %constant.140.clone.1, s32[]{:T(128)} %constant.140.clone.1, s32[]{:T(128)} %constant.140.clone.1, s32[]{:T(128)S(6)} %select_n.127) | dynamic-update-slice | bytes 393220 | tf_op jit(solution)/shard_map/dynamic_update_slice | solution.py:27
  111.6 5.6 %collective-permute-done.7 = bf16[2,1,64,1024]{3,2,0,1:T(8,128)(2,1)S(1)} collective-permute-done((bf16[2,1,64,1024]{3,2,0,1:T(8,128)(2,1)S(1)}, bf16[2,1,64,1024]{3,2,0,1:T(8,128)(2,1)S(1)}, u32[]{:S(2)}, u32[]{:S(2)}) %collective-permute-start.7) | collective-permute-done | bytes 262176 | tf_op jit(solution)/shard_map/ppermute | solution.py:20
  117.2 0.7 fusion.50
  118.1 5.8 %dynamic_update_slice.49 = bf16[2,1,768,1024]{3,2,0,1:T(8,128)(2,1)} dynamic-update-slice(bf16[2,1,768,1024]{3,2,0,1:T(8,128)(2,1)} %dynamic_update_slice.48, bf16[2,1,768,64]{3,2,0,1:T(8,128)(2,1)S(1)} %copy.6, s32[]{:T(128)} %constant.140.clone.1, s32[]{:T(128)} %constant.140.clone.1, s32[]{:T(128)} %constant.140.clone.1, s32[]{:T(128)S(6)} %select_n.129) | dynamic-update-slice | bytes 393220 | tf_op jit(solution)/shard_map/dynamic_update_slice | solution.py:27
  123.9 1.6 fusion.53
  125.7 4.9 %dynamic_update_slice.50 = bf16[2,1,768,1024]{3,2,0,1:T(8,128)(2,1)} dynamic-update-slice(bf16[2,1,768,1024]{3,2,0,1:T(8,128)(2,1)} %dynamic_update_slice.49, bf16[2,1,768,64]{3,2,0,1:T(8,128)(2,1)S(1)} %copy.7, s32[]{:T(128)} %constant.140.clone.1, s32[]{:T(128)} %constant.140.clone.1, s32[]{:T(128)} %constant.140.clone.1, s32[]{:T(128)S(6)} %select_n.131) | dynamic-update-slice | bytes 393220 | tf_op jit(solution)/shard_map/dynamic_update_slice | solution.py:27
  130.7 0.9 collective-permute-done.8
  131.6 1.6 fusion.56
  133.4 6.4 %dynamic_update_slice.51 = bf16[2,1,768,1024]{3,2,0,1:T(8,128)(2,1)} dynamic-update-slice(bf16[2,1,768,1024]{3,2,0,1:T(8,128)(2,1)} %dynamic_update_slice.50, bf16[2,1,768,64]{3,2,0,1:T(8,128)(2,1)S(1)} %copy.8, s32[]{:T(128)} %constant.140.clone.1, s32[]{:T(128)} %constant.140.clone.1, s32[]{:T(128)} %constant.140.clone.1, s32[]{:T(128)S(6)} %select_n.133) | dynamic-update-slice | bytes 393220 | tf_op jit(solution)/shard_map/dynamic_update_slice | solution.py:27
  140.7 5.5 %dynamic_update_slice.52 = bf16[2,1,768,1024]{3,2,0,1:T(8,128)(2,1)} dynamic-update-slice(bf16[2,1,768,1024]{3,2,0,1:T(8,128)(2,1)} %dynamic_update_slice.51, bf16[2,1,768,64]{3,2,0,1:T(8,128)(2,1)S(1)} %copy.9, s32[]{:T(128)} %constant.140.clone.1, s32[]{:T(128)} %constant.140.clone.1, s32[]{:T(128)} %constant.140.clone.1, s32[]{:T(128)S(6)} %select_n.135) | dynamic-update-slice | bytes 393220 | tf_op jit(solution)/shard_map/dynamic_update_slice | solution.py:27
  146.2 0.7 fusion.62
  147.1 6.4 %dynamic_update_slice.53 = bf16[2,1,768,1024]{3,2,0,1:T(8,128)(2,1)} dynamic-update-slice(bf16[2,1,768,1024]{3,2,0,1:T(8,128)(2,1)} %dynamic_update_slice.52, bf16[2,1,768,64]{3,2,0,1:T(8,128)(2,1)S(1)} %copy.10, s32[]{:T(128)} %constant.140.clone.1, s32[]{:T(128)} %constant.140.clone.1, s32[]{:T(128)} %constant.140.clone.1, s32[]{:T(128)S(6)} %select_n.137) | dynamic-update-slice | bytes 393220 | tf_op jit(solution)/shard_map/dynamic_update_slice | solution.py:27
  154.4 5.5 %dynamic_update_slice.54 = bf16[2,1,768,1024]{3,2,0,1:T(8,128)(2,1)} dynamic-update-slice(bf16[2,1,768,1024]{3,2,0,1:T(8,128)(2,1)} %dynamic_update_slice.53, bf16[2,1,768,64]{3,2,0,1:T(8,128)(2,1)S(1)} %copy.11, s32[]{:T(128)} %constant.140.clone.1, s32[]{:T(128)} %constant.140.clone.1, s32[]{:T(128)} %constant.140.clone.1, s32[]{:T(128)S(6)} %select_n.139) | dynamic-update-slice | bytes 393220 | tf_op jit(solution)/shard_map/dynamic_update_slice | solution.py:27
  159.9 0.8 collective-permute-done.10
  161.6 6.4 %dynamic_update_slice.55 = bf16[2,1,768,1024]{3,2,0,1:T(8,128)(2,1)} dynamic-update-slice(bf16[2,1,768,1024]{3,2,0,1:T(8,128)(2,1)} %dynamic_update_slice.54, bf16[2,1,768,64]{3,2,0,1:T(8,128)(2,1)S(1)} %copy.12, s32[]{:T(128)} %constant.140.clone.1, s32[]{:T(128)} %constant.140.clone.1, s32[]{:T(128)} %constant.140.clone.1, s32[]{:T(128)S(6)} %select_n.141) | dynamic-update-slice | bytes 393220 | tf_op jit(solution)/shard_map/dynamic_update_slice | solution.py:27
  168.8 5.5 %dynamic_update_slice.56 = bf16[2,1,768,1024]{3,2,0,1:T(8,128)(2,1)} dynamic-update-slice(bf16[2,1,768,1024]{3,2,0,1:T(8,128)(2,1)} %dynamic_update_slice.55, bf16[2,1,768,64]{3,2,0,1:T(8,128)(2,1)S(1)} %copy.13, s32[]{:T(128)} %constant.140.clone.1, s32[]{:T(128)} %constant.140.clone.1, s32[]{:T(128)} %constant.140.clone.1, s32[]{:T(128)S(6)} %select_n.143) | dynamic-update-slice | bytes 393220 | tf_op jit(solution)/shard_map/dynamic_update_slice | solution.py:27
  174.3 1.6 fusion.74
  176.2 6.3 %dynamic_update_slice.57 = bf16[2,1,768,1024]{3,2,0,1:T(8,128)(2,1)} dynamic-update-slice(bf16[2,1,768,1024]{3,2,0,1:T(8,128)(2,1)} %dynamic_update_slice.56, bf16[2,1,768,64]{3,2,0,1:T(8,128)(2,1)S(1)} %copy.14, s32[]{:T(128)} %constant.140.clone.1, s32[]{:T(128)} %constant.140.clone.1, s32[]{:T(128)} %constant.140.clone.1, s32[]{:T(128)S(6)} %select_n.145) | dynamic-update-slice | bytes 393220 | tf_op jit(solution)/shard_map/dynamic_update_slice | solution.py:27
  182.5 1.6 fusion.77
  184.3 5.5 %dynamic_update_slice.58 = bf16[2,1,768,1024]{3,2,0,1:T(8,128)(2,1)} dynamic-update-slice(bf16[2,1,768,1024]{3,2,0,1:T(8,128)(2,1)} %dynamic_update_slice.57, bf16[2,1,768,64]{3,2,0,1:T(8,128)(2,1)S(1)} %copy.15, s32[]{:T(128)} %constant.140.clone.1, s32[]{:T(128)} %constant.140.clone.1, s32[]{:T(128)} %constant.140.clone.1, s32[]{:T(128)S(6)} %select_n.147) | dynamic-update-slice | bytes 393220 | tf_op jit(solution)/shard_map/dynamic_update_slice | solution.py:27
  189.8 0.7 fusion.80
  190.7 6.3 %dynamic_update_slice.59 = bf16[2,1,768,1024]{3,2,0,1:T(8,128)(2,1)} dynamic-update-slice(bf16[2,1,768,1024]{3,2,0,1:T(8,128)(2,1)} %dynamic_update_slice.58, bf16[2,1,768,64]{3,2,0,1:T(8,128)(2,1)S(1)} %copy.16, s32[]{:T(128)} %constant.140.clone.1, s32[]{:T(128)} %constant.140.clone.1, s32[]{:T(128)} %constant.140.clone.1, s32[]{:T(128)S(6)} %select_n.149) | dynamic-update-slice | bytes 393220 | tf_op jit(solution)/shard_map/dynamic_update_slice | solution.py:27
  198.0 5.5 %dynamic_update_slice.60 = bf16[2,1,768,1024]{3,2,0,1:T(8,128)(2,1)} dynamic-update-slice(bf16[2,1,768,1024]{3,2,0,1:T(8,128)(2,1)} %dynamic_update_slice.59, bf16[2,1,768,64]{3,2,0,1:T(8,128)(2,1)S(1)} %copy.17, s32[]{:T(128)} %constant.140.clone.1, s32[]{:T(128)} %constant.140.clone.1, s32[]{:T(128)} %constant.140.clone.1, s32[]{:T(128)S(6)} %select_n.151) | dynamic-update-slice | bytes 393220 | tf_op jit(solution)/shard_map/dynamic_update_slice | solution.py:27
  204.3 6.4 %dynamic_update_slice.61 = bf16[2,1,768,1024]{3,2,0,1:T(8,128)(2,1)} dynamic-update-slice(bf16[2,1,768,1024]{3,2,0,1:T(8,128)(2,1)} %dynamic_update_slice.60, bf16[2,1,768,64]{3,2,0,1:T(8,128)(2,1)S(1)} %copy.18, s32[]{:T(128)} %constant.140.clone.1, s32[]{:T(128)} %constant.140.clone.1, s32[]{:T(128)} %constant.140.clone.1, s32[]{:T(128)S(6)} %select_n.153) | dynamic-update-slice | bytes 393220 | tf_op jit(solution)/shard_map/dynamic_update_slice | solution.py:27
  210.7 1.6 fusion.89
  212.5 5.5 %dynamic_update_slice.62 = bf16[2,1,768,1024]{3,2,0,1:T(8,128)(2,1)} dynamic-update-slice(bf16[2,1,768,1024]{3,2,0,1:T(8,128)(2,1)} %dynamic_update_slice.61, bf16[2,1,768,64]{3,2,0,1:T(8,128)(2,1)S(1)} %copy.19, s32[]{:T(128)} %constant.140.clone.1, s32[]{:T(128)} %constant.140.clone.1, s32[]{:T(128)} %constant.140.clone.1, s32[]{:T(128)S(6)} %select_n.155) | dynamic-update-slice | bytes 393220 | tf_op jit(solution)/shard_map/dynamic_update_slice | solution.py:27
  218.1 0.7 fusion.92
  219.0 6.3 %dynamic_update_slice.63 = bf16[2,1,768,1024]{3,2,0,1:T(8,128)(2,1)} dynamic-update-slice(bf16[2,1,768,1024]{3,2,0,1:T(8,128)(2,1)} %dynamic_update_slice.62, bf16[2,1,768,64]{3,2,0,1:T(8,128)(2,1)S(1)} %copy.20, s32[]{:T(128)} %constant.140.clone.1, s32[]{:T(128)} %constant.140.clone.1, s32[]{:T(128)} %constant.140.clone.1, s32[]{:T(128)S(6)} %select_n.157) | dynamic-update-slice | bytes 393220 | tf_op jit(solution)/shard_map/dynamic_update_slice | solution.py:27
  225.3 101.8 %while.14 = (s32[]{:T(128)}, f32[768,1024]{1,0:T(8,128)}, bf16[12288,1024]{1,0:T(8,128)(2,1)}, bf16[2,768,1024]{2,1,0:T(8,128)(2,1)}, s32[]{:T(128)}, /*index=5*/s32[]{:T(128)}, s32[]{:T(128)}, s32[]{:T(128)}) while((s32[]{:T(128)}, f32[768,1024]{1,0:T(8,128)}, bf16[12288,1024]{1,0:T(8,128)(2,1)}, bf16[2,768,1024]{2,1,0:T(8,128)(2,1)}, ...), condition=%wide.region_1.2_spmd.clone, body=%wide.region_0.1_spmd.clone.sunk | while | flops 9668395008 | bytes 68157656 | solution.py:69
  225.3 9.6 %convolution_bitcast_fusion.2 = f32[2,768,2048]{1,2,0:T(8,128)S(1)} fusion(bf16[2,768,1024]{2,1,0:T(8,128)(2,1)} %get-tuple-element.152, bf16[12288,1024]{1,0:T(8,128)(2,1)} %get-tuple-element.151, s32[]{:T(128)S(6)} %select_n.160), kind=kOutput, calls=%fused_computation.2.clone.1 | convolution fusion | flops 6442450944 | bytes 19922948 | tf_op jit(solution)/shard_map/while/body/eval_jaxpr/qoa,ba->qob/dot_general | solution.py:63
  234.9 5.7 %select_add_fusion.2 = f32[768,1024]{1,0:T(8,128)S(1)} fusion(f32[768,1024]{1,0:T(8,128)S(1)} %copy-done.10, bf16[12288,1024]{1,0:T(8,128)(2,1)} %get-tuple-element.151, s32[]{:T(128)S(6)} %select_n.160, f32[2,768,2048]{1,2,0:T(8,128)S(1)} %convolution_bitcast_fusion.2, pred[]{:T(512)S(6)} %compare.19), kind=kOutput, calls=%fused_computation.8.clone.1 | convolution fusion | flops 3225944064 | bytes 23068676 | tf_op jit(solution)/shard_map/while/body/eval_jaxpr/dot_general | solution.py:67
  240.6 1.7 copy-done.11
  242.3 9.6 %convolution_bitcast_fusion.2 = f32[2,768,2048]{1,2,0:T(8,128)S(1)} fusion(bf16[2,768,1024]{2,1,0:T(8,128)(2,1)} %get-tuple-element.152, bf16[12288,1024]{1,0:T(8,128)(2,1)} %get-tuple-element.151, s32[]{:T(128)S(6)} %select_n.160), kind=kOutput, calls=%fused_computation.2.clone.1 | convolution fusion | flops 6442450944 | bytes 19922948 | tf_op jit(solution)/shard_map/while/body/eval_jaxpr/qoa,ba->qob/dot_general | solution.py:63
  251.9 5.7 %select_add_fusion.2 = f32[768,1024]{1,0:T(8,128)S(1)} fusion(f32[768,1024]{1,0:T(8,128)S(1)} %copy-done.10, bf16[12288,1024]{1,0:T(8,128)(2,1)} %get-tuple-element.151, s32[]{:T(128)S(6)} %select_n.160, f32[2,768,2048]{1,2,0:T(8,128)S(1)} %convolution_bitcast_fusion.2, pred[]{:T(512)S(6)} %compare.19), kind=kOutput, calls=%fused_computation.8.clone.1 | convolution fusion | flops 3225944064 | bytes 23068676 | tf_op jit(solution)/shard_map/while/body/eval_jaxpr/dot_general | solution.py:67
  257.6 1.7 copy-done.11
  259.3 9.6 %convolution_bitcast_fusion.2 = f32[2,768,2048]{1,2,0:T(8,128)S(1)} fusion(bf16[2,768,1024]{2,1,0:T(8,128)(2,1)} %get-tuple-element.152, bf16[12288,1024]{1,0:T(8,128)(2,1)} %get-tuple-element.151, s32[]{:T(128)S(6)} %select_n.160), kind=kOutput, calls=%fused_computation.2.clone.1 | convolution fusion | flops 6442450944 | bytes 19922948 | tf_op jit(solution)/shard_map/while/body/eval_jaxpr/qoa,ba->qob/dot_general | solution.py:63
  268.9 5.7 %select_add_fusion.2 = f32[768,1024]{1,0:T(8,128)S(1)} fusion(f32[768,1024]{1,0:T(8,128)S(1)} %copy-done.10, bf16[12288,1024]{1,0:T(8,128)(2,1)} %get-tuple-element.151, s32[]{:T(128)S(6)} %select_n.160, f32[2,768,2048]{1,2,0:T(8,128)S(1)} %convolution_bitcast_fusion.2, pred[]{:T(512)S(6)} %compare.19), kind=kOutput, calls=%fused_computation.8.clone.1 | convolution fusion | flops 3225944064 | bytes 23068676 | tf_op jit(solution)/shard_map/while/body/eval_jaxpr/dot_general | solution.py:67
  274.5 1.7 copy-done.11
  276.2 9.6 %convolution_bitcast_fusion.2 = f32[2,768,2048]{1,2,0:T(8,128)S(1)} fusion(bf16[2,768,1024]{2,1,0:T(8,128)(2,1)} %get-tuple-element.152, bf16[12288,1024]{1,0:T(8,128)(2,1)} %get-tuple-element.151, s32[]{:T(128)S(6)} %select_n.160), kind=kOutput, calls=%fused_computation.2.clone.1 | convolution fusion | flops 6442450944 | bytes 19922948 | tf_op jit(solution)/shard_map/while/body/eval_jaxpr/qoa,ba->qob/dot_general | solution.py:63
  285.8 5.7 %select_add_fusion.2 = f32[768,1024]{1,0:T(8,128)S(1)} fusion(f32[768,1024]{1,0:T(8,128)S(1)} %copy-done.10, bf16[12288,1024]{1,0:T(8,128)(2,1)} %get-tuple-element.151, s32[]{:T(128)S(6)} %select_n.160, f32[2,768,2048]{1,2,0:T(8,128)S(1)} %convolution_bitcast_fusion.2, pred[]{:T(512)S(6)} %compare.19), kind=kOutput, calls=%fused_computation.8.clone.1 | convolution fusion | flops 3225944064 | bytes 23068676 | tf_op jit(solution)/shard_map/while/body/eval_jaxpr/dot_general | solution.py:67
  291.5 1.7 copy-done.11
  293.2 9.6 %convolution_bitcast_fusion.2 = f32[2,768,2048]{1,2,0:T(8,128)S(1)} fusion(bf16[2,768,1024]{2,1,0:T(8,128)(2,1)} %get-tuple-element.152, bf16[12288,1024]{1,0:T(8,128)(2,1)} %get-tuple-element.151, s32[]{:T(128)S(6)} %select_n.160), kind=kOutput, calls=%fused_computation.2.clone.1 | convolution fusion | flops 6442450944 | bytes 19922948 | tf_op jit(solution)/shard_map/while/body/eval_jaxpr/qoa,ba->qob/dot_general | solution.py:63
  302.8 5.7 %select_add_fusion.2 = f32[768,1024]{1,0:T(8,128)S(1)} fusion(f32[768,1024]{1,0:T(8,128)S(1)} %copy-done.10, bf16[12288,1024]{1,0:T(8,128)(2,1)} %get-tuple-element.151, s32[]{:T(128)S(6)} %select_n.160, f32[2,768,2048]{1,2,0:T(8,128)S(1)} %convolution_bitcast_fusion.2, pred[]{:T(512)S(6)} %compare.19), kind=kOutput, calls=%fused_computation.8.clone.1 | convolution fusion | flops 3225944064 | bytes 23068676 | tf_op jit(solution)/shard_map/while/body/eval_jaxpr/dot_general | solution.py:67
  308.5 1.7 copy-done.11
  310.2 9.6 %convolution_bitcast_fusion.2 = f32[2,768,2048]{1,2,0:T(8,128)S(1)} fusion(bf16[2,768,1024]{2,1,0:T(8,128)(2,1)} %get-tuple-element.152, bf16[12288,1024]{1,0:T(8,128)(2,1)} %get-tuple-element.151, s32[]{:T(128)S(6)} %select_n.160), kind=kOutput, calls=%fused_computation.2.clone.1 | convolution fusion | flops 6442450944 | bytes 19922948 | tf_op jit(solution)/shard_map/while/body/eval_jaxpr/qoa,ba->qob/dot_general | solution.py:63
  319.8 5.7 %select_add_fusion.2 = f32[768,1024]{1,0:T(8,128)S(1)} fusion(f32[768,1024]{1,0:T(8,128)S(1)} %copy-done.10, bf16[12288,1024]{1,0:T(8,128)(2,1)} %get-tuple-element.151, s32[]{:T(128)S(6)} %select_n.160, f32[2,768,2048]{1,2,0:T(8,128)S(1)} %convolution_bitcast_fusion.2, pred[]{:T(512)S(6)} %compare.19), kind=kOutput, calls=%fused_computation.8.clone.1 | convolution fusion | flops 3225944064 | bytes 23068676 | tf_op jit(solution)/shard_map/while/body/eval_jaxpr/dot_general | solution.py:67
  325.5 1.7 copy-done.11
  327.1 5.7 %fusion.45 = f32[1024,1024]{1,0:T(8,128)} fusion(bf16[768,1024]{1,0:T(8,128)(2,1)S(1)} %copy-done.1, f32[768,1024]{1,0:T(8,128)} %get-tuple-element.84), kind=kOutput, calls=%fused_computation.44 | convolution fusion | flops 1611399168 | bytes 8912896 | tf_op jit(solution)/shard_map/tsk,sl->ktl/dot_general | solution.py:85
  333.1 75.7 %reduce-scatter.3.cloned.1.call-done = f32[64,1024]{1,0:T(8,128)} async-done(((f32[1024,1024]{1,0:T(8,128)}), f32[64,1024]{1,0:T(8,128)}) %reduce-scatter.3.cloned.1.call-update) | async-done | bytes 262160 | tf_op jit(solution)/shard_map/reduce_scatter | solution.py:84
  408.8 1.9 multiply_multiply_fusion
  410.8 14.1 %reduce-scatter.5.cloned.1.call-done = f32[1,64,1024]{2,1,0:T(8,128)} async-done(((f32[2,64,1024]{2,1,0:T(8,128)}), f32[1,64,1024]{2,1,0:T(8,128)}) %reduce-scatter.5.cloned.1.call-update) | async-done | bytes 262160 | tf_op jit(solution)/shard_map/reduce_scatter | solution.py:93
  (86 shorter events, 8.4 us)
Async XLA Ops:
  6.5 326.4 %copy-start = (f32[2,2]{1,0:T(2,128)S(1)}, f32[2,2]{1,0:T(2,128)}, u32[]{:S(2)}) copy-start(f32[2,2]{1,0:T(2,128)} %param.9) | copy-start | bytes 52
  6.5 96.5 %copy-start.1 = (bf16[768,1024]{1,0:T(8,128)(2,1)S(1)}, bf16[768,1024]{1,0:T(8,128)(2,1)}, u32[]{:S(2)}) copy-start(bf16[768,1024]{1,0:T(8,128)(2,1)} %param.8) | copy-start | bytes 4718596
  6.5 96.5 %copy-start.2 = (bf16[1,64,1024]{2,1,0:T(8,128)(2,1)S(1)}, bf16[1,64,1024]{2,1,0:T(8,128)(2,1)}, u32[]{:S(2)}) copy-start(bf16[1,64,1024]{2,1,0:T(8,128)(2,1)} %param.7) | copy-start | bytes 393220
  6.5 96.5 %copy-start.3 = (bf16[1,64,1024]{2,1,0:T(8,128)(2,1)S(1)}, bf16[1,64,1024]{2,1,0:T(8,128)(2,1)}, u32[]{:S(2)}) copy-start(bf16[1,64,1024]{2,1,0:T(8,128)(2,1)} %param.6) | copy-start | bytes 393220
  6.5 218.8 %all-gather.2.cloned.1.call-start = ((), (), s32[]{:S(2)}) async-start(), calls=%async_computation.2 | async-start | bytes 26738688 | tf_op jit(solution)/shard_map/all_gather | solution.py:82
  7.3 401.6 %reduce-scatter.3.cloned.1.call-start = ((), (), s32[]{:S(2)}) async-start(), calls=%async_computation.3 | async-start | bytes 4456448 | tf_op jit(solution)/shard_map/reduce_scatter | solution.py:84
  8.3 9.6 %collective-permute-start = (bf16[2,1,64,1024]{3,2,0,1:T(8,128)(2,1)S(1)}, bf16[2,1,64,1024]{3,2,0,1:T(8,128)(2,1)S(1)}, u32[]{:S(2)}, u32[]{:S(2)}) collective-permute-start(bf16[2,1,64,1024]{3,2,0,1:T(8,128)(2,1)S(1)} %pad_maximum_fusion), channel_id=1, source_target_pairs={{0,1},{1,2},{2,3},{3,4},{4,5},{5,6},{6,7},{7,8},{8,9},{9,10},{10,1... | collective-permute-start | bytes 786440 | tf_op jit(solution)/shard_map/ppermute | solution.py:20
  17.9 0.7 copy-start.7
  17.9 13.9 %collective-permute-start.1 = (bf16[2,1,64,1024]{3,2,0,1:T(8,128)(2,1)S(1)}, bf16[2,1,64,1024]{3,2,0,1:T(8,128)(2,1)S(1)}, u32[]{:S(2)}, u32[]{:S(2)}) collective-permute-start(bf16[2,1,64,1024]{3,2,0,1:T(8,128)(2,1)S(1)} %collective-permute-done), channel_id=1, source_target_pairs={{0,1},{1,2},{2,3},{3,4},{4,5},{5,6},{6,7},{7,8},{8,9},{9,10},{10,1... | collective-permute-start | bytes 786440 | tf_op jit(solution)/shard_map/ppermute | solution.py:20
  31.8 0.7 copy-start.9
  31.8 14.2 %collective-permute-start.2 = (bf16[2,1,64,1024]{3,2,0,1:T(8,128)(2,1)S(1)}, bf16[2,1,64,1024]{3,2,0,1:T(8,128)(2,1)S(1)}, u32[]{:S(2)}, u32[]{:S(2)}) collective-permute-start(bf16[2,1,64,1024]{3,2,0,1:T(8,128)(2,1)S(1)} %collective-permute-done.1), channel_id=1, source_target_pairs={{0,1},{1,2},{2,3},{3,4},{4,5},{5,6},{6,7},{7,8},{8,9},{9,10},{10,1... | collective-permute-start | bytes 786440 | tf_op jit(solution)/shard_map/ppermute | solution.py:20
  46.0 28.5 %copy-start.6 = (bf16[2,1,64,1024]{3,2,0,1:T(8,128)(2,1)}, bf16[2,1,64,1024]{3,2,0,1:T(8,128)(2,1)S(1)}, u32[]{:S(2)}) copy-start(bf16[2,1,64,1024]{3,2,0,1:T(8,128)(2,1)S(1)} %collective-permute-done.2) | copy-start | bytes 786436
  46.0 14.2 %collective-permute-start.3 = (bf16[2,1,64,1024]{3,2,0,1:T(8,128)(2,1)S(1)}, bf16[2,1,64,1024]{3,2,0,1:T(8,128)(2,1)S(1)}, u32[]{:S(2)}, u32[]{:S(2)}) collective-permute-start(bf16[2,1,64,1024]{3,2,0,1:T(8,128)(2,1)S(1)} %collective-permute-done.2), channel_id=1, source_target_pairs={{0,1},{1,2},{2,3},{3,4},{4,5},{5,6},{6,7},{7,8},{8,9},{9,10},{10,1... | collective-permute-start | bytes 786440 | tf_op jit(solution)/shard_map/ppermute | solution.py:20
  60.3 28.5 %copy-start.4 = (bf16[2,1,64,1024]{3,2,0,1:T(8,128)(2,1)}, bf16[2,1,64,1024]{3,2,0,1:T(8,128)(2,1)S(1)}, u32[]{:S(2)}) copy-start(bf16[2,1,64,1024]{3,2,0,1:T(8,128)(2,1)S(1)} %collective-permute-done.3) | copy-start | bytes 786436
  60.3 14.2 %collective-permute-start.4 = (bf16[2,1,64,1024]{3,2,0,1:T(8,128)(2,1)S(1)}, bf16[2,1,64,1024]{3,2,0,1:T(8,128)(2,1)S(1)}, u32[]{:S(2)}, u32[]{:S(2)}) collective-permute-start(bf16[2,1,64,1024]{3,2,0,1:T(8,128)(2,1)S(1)} %collective-permute-done.3), channel_id=1, source_target_pairs={{0,1},{1,2},{2,3},{3,4},{4,5},{5,6},{6,7},{7,8},{8,9},{9,10},{10,1... | collective-permute-start | bytes 786440 | tf_op jit(solution)/shard_map/ppermute | solution.py:20
  74.5 14.2 %collective-permute-start.5 = (bf16[2,1,64,1024]{3,2,0,1:T(8,128)(2,1)S(1)}, bf16[2,1,64,1024]{3,2,0,1:T(8,128)(2,1)S(1)}, u32[]{:S(2)}, u32[]{:S(2)}) collective-permute-start(bf16[2,1,64,1024]{3,2,0,1:T(8,128)(2,1)S(1)} %collective-permute-done.4), channel_id=1, source_target_pairs={{0,1},{1,2},{2,3},{3,4},{4,5},{5,6},{6,7},{7,8},{8,9},{9,10},{10,1... | collective-permute-start | bytes 786440 | tf_op jit(solution)/shard_map/ppermute | solution.py:20
  88.7 14.2 %collective-permute-start.6 = (bf16[2,1,64,1024]{3,2,0,1:T(8,128)(2,1)S(1)}, bf16[2,1,64,1024]{3,2,0,1:T(8,128)(2,1)S(1)}, u32[]{:S(2)}, u32[]{:S(2)}) collective-permute-start(bf16[2,1,64,1024]{3,2,0,1:T(8,128)(2,1)S(1)} %collective-permute-done.5), channel_id=1, source_target_pairs={{0,1},{1,2},{2,3},{3,4},{4,5},{5,6},{6,7},{7,8},{8,9},{9,10},{10,1... | collective-permute-start | bytes 786440 | tf_op jit(solution)/shard_map/ppermute | solution.py:20
  103.0 14.2 %collective-permute-start.7 = (bf16[2,1,64,1024]{3,2,0,1:T(8,128)(2,1)S(1)}, bf16[2,1,64,1024]{3,2,0,1:T(8,128)(2,1)S(1)}, u32[]{:S(2)}, u32[]{:S(2)}) collective-permute-start(bf16[2,1,64,1024]{3,2,0,1:T(8,128)(2,1)S(1)} %collective-permute-done.6), channel_id=1, source_target_pairs={{0,1},{1,2},{2,3},{3,4},{4,5},{5,6},{6,7},{7,8},{8,9},{9,10},{10,1... | collective-permute-start | bytes 786440 | tf_op jit(solution)/shard_map/ppermute | solution.py:20
  104.0 13.2 %copy-start.8 = (bf16[2,1,64,1024]{3,2,0,1:T(8,128)(2,1)S(1)}, bf16[2,1,64,1024]{3,2,0,1:T(8,128)(2,1)}, u32[]{:S(2)}) copy-start(bf16[2,1,64,1024]{3,2,0,1:T(8,128)(2,1)} %copy-done.7) | copy-start | bytes 786436
  117.2 14.3 %collective-permute-start.8 = (bf16[2,1,64,1024]{3,2,0,1:T(8,128)(2,1)S(1)}, bf16[2,1,64,1024]{3,2,0,1:T(8,128)(2,1)}, u32[]{:S(2)}, u32[]{:S(2)}) collective-permute-start(bf16[2,1,64,1024]{3,2,0,1:T(8,128)(2,1)S(1)} %collective-permute-done.7), channel_id=1, source_target_pairs={{0,1},{1,2},{2,3},{3,4},{4,5},{5,6},{6,7},{7,8},{8,9},{9,10},{10,1... | collective-permute-start | bytes 786440 | tf_op jit(solution)/shard_map/ppermute | solution.py:20
  130.7 9.1 %copy-start.5 = (bf16[2,1,64,1024]{3,2,0,1:T(8,128)(2,1)S(1)}, bf16[2,1,64,1024]{3,2,0,1:T(8,128)(2,1)}, u32[]{:S(2)}) copy-start(bf16[2,1,64,1024]{3,2,0,1:T(8,128)(2,1)} %copy-done.4) | copy-start | bytes 786436
  131.6 14.7 %collective-permute-start.9 = (bf16[2,1,64,1024]{3,2,0,1:T(8,128)(2,1)}, bf16[2,1,64,1024]{3,2,0,1:T(8,128)(2,1)}, u32[]{:S(2)}, u32[]{:S(2)}) collective-permute-start(bf16[2,1,64,1024]{3,2,0,1:T(8,128)(2,1)} %collective-permute-done.8), channel_id=1, source_target_pairs={{0,1},{1,2},{2,3},{3,4},{4,5},{5,6},{6,7},{7,8},{8,9},{9,10},{10,1... | collective-permute-start | bytes 786440 | tf_op jit(solution)/shard_map/ppermute | solution.py:20
  146.2 14.5 %collective-permute-start.10 = (bf16[2,1,64,1024]{3,2,0,1:T(8,128)(2,1)}, bf16[2,1,64,1024]{3,2,0,1:T(8,128)(2,1)S(1)}, u32[]{:S(2)}, u32[]{:S(2)}) collective-permute-start(bf16[2,1,64,1024]{3,2,0,1:T(8,128)(2,1)} %collective-permute-done.9), channel_id=1, source_target_pairs={{0,1},{1,2},{2,3},{3,4},{4,5},{5,6},{6,7},{7,8},{8,9},{9,10},{10,1... | collective-permute-start | bytes 786440 | tf_op jit(solution)/shard_map/ppermute | solution.py:20
  160.7 13.6 %collective-permute-start.11 = (bf16[2,1,64,1024]{3,2,0,1:T(8,128)(2,1)S(1)}, bf16[2,1,64,1024]{3,2,0,1:T(8,128)(2,1)S(1)}, u32[]{:S(2)}, u32[]{:S(2)}) collective-permute-start(bf16[2,1,64,1024]{3,2,0,1:T(8,128)(2,1)S(1)} %collective-permute-done.10), channel_id=1, source_target_pairs={{0,1},{1,2},{2,3},{3,4},{4,5},{5,6},{6,7},{7,8},{8,9},{9,10},{10,1... | collective-permute-start | bytes 786440 | tf_op jit(solution)/shard_map/ppermute | solution.py:20
  174.3 15.5 %collective-permute-start.12 = (bf16[2,1,64,1024]{3,2,0,1:T(8,128)(2,1)S(1)}, bf16[2,1,64,1024]{3,2,0,1:T(8,128)(2,1)S(1)}, u32[]{:S(2)}, u32[]{:S(2)}) collective-permute-start(bf16[2,1,64,1024]{3,2,0,1:T(8,128)(2,1)S(1)} %collective-permute-done.11), channel_id=1, source_target_pairs={{0,1},{1,2},{2,3},{3,4},{4,5},{5,6},{6,7},{7,8},{8,9},{9,10},{10,1... | collective-permute-start | bytes 786440 | tf_op jit(solution)/shard_map/ppermute | solution.py:20
  189.8 13.6 %collective-permute-start.13 = (bf16[2,1,64,1024]{3,2,0,1:T(8,128)(2,1)S(1)}, bf16[2,1,64,1024]{3,2,0,1:T(8,128)(2,1)}, u32[]{:S(2)}, u32[]{:S(2)}) collective-permute-start(bf16[2,1,64,1024]{3,2,0,1:T(8,128)(2,1)S(1)} %collective-permute-done.12), channel_id=1, source_target_pairs={{0,1},{1,2},{2,3},{3,4},{4,5},{5,6},{6,7},{7,8},{8,9},{9,10},{10,1... | collective-permute-start | bytes 786440 | tf_op jit(solution)/shard_map/ppermute | solution.py:20
  203.5 14.6 %collective-permute-start.14 = (bf16[2,1,64,1024]{3,2,0,1:T(8,128)(2,1)}, bf16[2,1,64,1024]{3,2,0,1:T(8,128)(2,1)S(1)}, u32[]{:S(2)}, u32[]{:S(2)}) collective-permute-start(bf16[2,1,64,1024]{3,2,0,1:T(8,128)(2,1)} %collective-permute-done.13), channel_id=1, source_target_pairs={{0,1},{1,2},{2,3},{3,4},{4,5},{5,6},{6,7},{7,8},{8,9},{9,10},{10,1... | collective-permute-start | bytes 786440 | tf_op jit(solution)/shard_map/ppermute | solution.py:20
  225.3 9.6 %copy-start.10 = (f32[768,1024]{1,0:T(8,128)S(1)}, f32[768,1024]{1,0:T(8,128)}, u32[]{:S(2)}) copy-start(f32[768,1024]{1,0:T(8,128)} %get-tuple-element.142) | copy-start | bytes 9437188 | tf_op jit(solution)/shard_map/while
  240.6 1.7 copy-start.11
  242.3 9.6 %copy-start.10 = (f32[768,1024]{1,0:T(8,128)S(1)}, f32[768,1024]{1,0:T(8,128)}, u32[]{:S(2)}) copy-start(f32[768,1024]{1,0:T(8,128)} %get-tuple-element.142) | copy-start | bytes 9437188 | tf_op jit(solution)/shard_map/while
  257.6 1.7 copy-start.11
  259.3 9.6 %copy-start.10 = (f32[768,1024]{1,0:T(8,128)S(1)}, f32[768,1024]{1,0:T(8,128)}, u32[]{:S(2)}) copy-start(f32[768,1024]{1,0:T(8,128)} %get-tuple-element.142) | copy-start | bytes 9437188 | tf_op jit(solution)/shard_map/while
  274.5 1.7 copy-start.11
  276.2 9.6 %copy-start.10 = (f32[768,1024]{1,0:T(8,128)S(1)}, f32[768,1024]{1,0:T(8,128)}, u32[]{:S(2)}) copy-start(f32[768,1024]{1,0:T(8,128)} %get-tuple-element.142) | copy-start | bytes 9437188 | tf_op jit(solution)/shard_map/while
  291.5 1.7 copy-start.11
  293.2 9.6 %copy-start.10 = (f32[768,1024]{1,0:T(8,128)S(1)}, f32[768,1024]{1,0:T(8,128)}, u32[]{:S(2)}) copy-start(f32[768,1024]{1,0:T(8,128)} %get-tuple-element.142) | copy-start | bytes 9437188 | tf_op jit(solution)/shard_map/while
  308.5 1.7 copy-start.11
  310.2 9.6 %copy-start.10 = (f32[768,1024]{1,0:T(8,128)S(1)}, f32[768,1024]{1,0:T(8,128)}, u32[]{:S(2)}) copy-start(f32[768,1024]{1,0:T(8,128)} %get-tuple-element.142) | copy-start | bytes 9437188 | tf_op jit(solution)/shard_map/while
  325.4 1.7 copy-start.11
  332.9 91.9 %reduce-scatter.5.cloned.1.call-start = ((), (), s32[]{:S(2)}) async-start(), calls=%async_computation.4 | async-start | bytes 786432 | tf_op jit(solution)/shard_map/reduce_scatter | solution.py:93
Sparse Core Ops, SparseCore 0:
  8.9 159.3 all-gather.1
  333.0 75.7 reduce-scatter.2
  411.1 13.6 reduce-scatter.4
